TPU v7x, 256 devices: a whole 4x4x8 slice. The times are simulated.
256 devices in a mesh: seq: 16 (over x, y), fsdp: 16 (over z, core).
Axes of the slice: x: 4, y: 4, z: 8, core: 2. Of those that a mesh axis runs over, the one named last changes fastest.
Arguments:
- patches: bfloat16 [16, 8704, 1176], P('fsdp', 'seq'), may hold values from -6 to 6
- send_slot: int32 [16, 272], P('fsdp', 'seq'), may hold values from 0 to 271, as said below
- segments: int32 [16, 272], P('fsdp'), may hold values from 0 to 33, never falling along the last dimension, each value on 1 to 24 neighbouring positions
- stem_weight: bfloat16 [3584, 1176], P('fsdp'), may hold values from -0.1875 to 0.1875
- norm_gain: bfloat16 [3584], P('fsdp'), may hold values from 0.099609375 to 1.8984375
- conv_kernel: bfloat16 [5, 3584], P(None, 'fsdp'), may hold values from -3 to 3
- cotangent: bfloat16 [16, 8704, 3584], P('fsdp', 'seq'), may hold values from -6 to 6
Outputs:
- features: bfloat16 [16, 8704, 3584], P('fsdp', 'seq')
- grad_patches: bfloat16 [16, 8704, 1176], P('fsdp', 'seq')
- grad_weight: bfloat16 [3584, 1176], P('fsdp')
- grad_channels: float32 [6, 3584], P(None, 'fsdp')
Inputs may be any that keep to these rules, and one draw needn't show every extreme that they name: `send_slot`: each row is a permutation of the packed slots. At most 2 frame slots of one device go to one device's packed slots, and every device sends exactly 2 to some device; within a row the number that device s sends to device (s + o) modulo the seq axis size depends on o alone. `segments`: ids never fall along a row; a clip holds 1 to 24 slots, one exactly 24.
All inputs are finite; a program needn't handle non-finite values.
Results may differ from a plain program's by a relative error of at most 0.0056.
Values may be sent and summed in bfloat16 or wider, within the bound.
A program may use at most 192 MiB of HBM per device.

v0:
```python
import math
import jax
import jax.numpy as jnp
from jax import lax
from jax.sharding import PartitionSpec as P

EPSILON = 1e-06


def extended_2(cells, sides, width):
    for axis, dim in sides:
        count = lax.axis_size(axis)
        ends = count - 1
        head = lax.slice_in_dim(cells, 0, width, axis=dim)
        tail = lax.slice_in_dim(cells, cells.shape[dim] - width, cells.shape[dim], axis=dim)
        cells = jnp.concatenate(
            [
                lax.ppermute(tail, axis, [(i, (i + 1) % count) for i in range(ends)]),
                cells,
                lax.ppermute(head, axis, [((i + 1) % count, i) for i in range(ends)]),
            ],
            axis=dim,
        )
    return cells


def slot_mask(segment_row, centre):
    slot_total = segment_row.shape[0]
    safe_centre = jnp.clip(centre, 0, slot_total - 1)
    columns = []
    for offset in range(5):
        neighbour = centre + (offset - 2)
        inside = (neighbour >= 0) & (neighbour < slot_total) & (centre >= 0) & (centre < slot_total)
        same_clip = segment_row[jnp.clip(neighbour, 0, slot_total - 1)] == segment_row[safe_centre]
        columns.append((inside & same_clip).astype(jnp.float32))
    return jnp.stack(columns, axis=1)


def temporal_mix(padded, clip_mask, kernel, slot_total):
    kernel_wide = kernel.astype(jnp.float32)
    result = padded[0:slot_total].astype(jnp.float32) * (
        clip_mask[:, 0][:, None, None] * kernel_wide[0][None, None, :]
    )
    for offset in range(1, 5):
        addend = padded[offset : offset + slot_total].astype(jnp.float32) * (
            clip_mask[:, offset][:, None, None] * kernel_wide[offset][None, None, :]
        )
        result = result + addend
    return result


def temporal_back(slope_padded, mask_padded, kernel, slot_total):
    kernel_wide = kernel.astype(jnp.float32)
    result = jnp.zeros((slot_total,) + slope_padded.shape[1:], jnp.float32)
    for offset in range(5):
        first_row = 4 - offset
        weights_row = (
            mask_padded[first_row : first_row + slot_total, offset][:, None, None]
            * kernel_wide[offset][None, None, :]
        )
        result = (
            result
            + slope_padded[first_row : first_row + slot_total].astype(jnp.float32) * weights_row
        )
    return result


def kernel_sums(slope_blocks, padded, clip_mask, slot_total):
    stacked = []
    for offset in range(5):
        product = jnp.sum(
            slope_blocks.astype(jnp.float32)
            * padded[offset : offset + slot_total].astype(jnp.float32),
            axis=1,
        )
        stacked.append(jnp.sum(product * clip_mask[:, offset][:, None], axis=0))
    return jnp.stack(stacked, axis=0)


def rim_rows(values, margin):
    return extended_2(values, (("seq", 0),), margin)


def shards(patches, send_slot, segments, stem_weight, norm_gain, conv_kernel, cotangent):
    seq_size = lax.axis_size("seq")
    fsdp_size = lax.axis_size("fsdp")
    seq_index = lax.axis_index("seq")
    slot_count = send_slot.shape[1]
    tokens = patches.shape[1]
    slot_rows = tokens // slot_count
    pixel_width = patches.shape[2]
    capacity = 2 * slot_count // seq_size
    destination = send_slot[0]
    owner_index = destination // slot_count
    same_owner = owner_index[:, None] == owner_index[None, :]
    earlier = destination[None, :] < destination[:, None]
    ranking = jnp.sum((same_owner & earlier).astype(jnp.int32), axis=1)
    buffer_row = owner_index * capacity + ranking
    frames = patches[0].reshape(slot_count, slot_rows, pixel_width)
    outbox = (
        jnp.zeros((seq_size * capacity, slot_rows, pixel_width), jnp.bfloat16)
        .at[buffer_row]
        .set(frames)
    )
    position = (
        jnp.full((seq_size * capacity,), -1.0, jnp.float32)
        .at[buffer_row]
        .set((destination % slot_count).astype(jnp.float32))
        .astype(jnp.bfloat16)
    )
    incoming, arrived = (
        lax.all_to_all(outbox, "seq", split_axis=0, concat_axis=0, tiled=True),
        lax.all_to_all(position, "seq", split_axis=0, concat_axis=0, tiled=True),
    )
    arrived_float = arrived.astype(jnp.float32)
    target = jnp.where(arrived_float >= 0.0, arrived_float, float(slot_count)).astype(jnp.int32)
    packed = (
        jnp.zeros((slot_count + 1, slot_rows, pixel_width), jnp.bfloat16)
        .at[target]
        .set(incoming)[:slot_count]
        .reshape(tokens, pixel_width)
    )
    weight_full, gain_low, kernel_full = (
        lax.all_gather(stem_weight, "fsdp", axis=0, tiled=True),
        lax.all_gather(norm_gain, "fsdp", axis=0, tiled=True),
        lax.all_gather(conv_kernel, "fsdp", axis=1, tiled=True),
    )
    gain_wide = gain_low.astype(jnp.float32)
    channels = weight_full.shape[0]
    stem_out = lax.dot_general(
        packed, weight_full, (((1,), (1,)), ((), ())), preferred_element_type=jnp.float32
    )
    inv_rms = lax.rsqrt(jnp.mean(stem_out * stem_out, axis=1, keepdims=True) + EPSILON)
    unit_rows = stem_out * inv_rms
    normed = (unit_rows * gain_wide).astype(jnp.bfloat16)
    segment_row = segments[0]
    centre = seq_index * slot_count + jnp.arange(slot_count, dtype=jnp.int32)
    extended = seq_index * slot_count + jnp.arange(-2, slot_count + 2, dtype=jnp.int32)
    clip_mask = slot_mask(segment_row, centre)
    mask_padded = slot_mask(segment_row, extended)
    padded = rim_rows(normed, 2 * slot_rows).reshape(slot_count + 4, slot_rows, channels)
    mixed_rows = temporal_mix(padded, clip_mask, kernel_full, slot_count).reshape(tokens, channels)
    features = (stem_out + jax.nn.silu(mixed_rows)).astype(jnp.bfloat16)
    upstream_wide = cotangent[0].astype(jnp.float32)
    gate_value = jax.nn.sigmoid(mixed_rows)
    slope_low = (upstream_wide * gate_value * (1.0 + mixed_rows * (1.0 - gate_value))).astype(
        jnp.bfloat16
    )
    slope_padded = rim_rows(slope_low, 2 * slot_rows).reshape(slot_count + 4, slot_rows, channels)
    d_normed = temporal_back(slope_padded, mask_padded, kernel_full, slot_count).reshape(
        tokens, channels
    )
    gated = d_normed * gain_wide
    d_stem = upstream_wide + inv_rms * (
        gated - unit_rows * jnp.mean(gated * unit_rows, axis=1, keepdims=True)
    )
    d_stem_low = d_stem.astype(jnp.bfloat16)
    grad_rows = jnp.dot(d_stem_low, weight_full, preferred_element_type=jnp.float32).astype(
        jnp.bfloat16
    )
    gain_part = jnp.sum(d_normed * unit_rows, axis=0)
    slope_blocks = slope_padded[2 : 2 + slot_count]
    kernel_part = kernel_sums(slope_blocks, padded, clip_mask, slot_count)
    chan_terms = jnp.concatenate([gain_part[None, :], kernel_part], axis=0).T
    weight_block = lax.dot_general(
        d_stem_low, packed, (((0,), (0,)), ((), ())), preferred_element_type=jnp.float32
    )
    grad_shard = lax.psum_scatter(
        jnp.concatenate([weight_block, chan_terms], axis=1), "fsdp", scatter_dimension=0, tiled=True
    )
    summed = lax.psum(grad_shard, "seq")
    grad_scale = 1.0 / math.sqrt(tokens * seq_size * fsdp_size)
    grad_weight = (summed[:, :pixel_width] * grad_scale).astype(jnp.bfloat16)
    grad_channels = (summed[:, pixel_width:] * grad_scale).T
    return (features[None], grad_rows[None], grad_weight, grad_channels)


def solution(mesh):
    in_specs = (
        P("fsdp", "seq", None),
        P("fsdp", "seq"),
        P("fsdp", None),
        P("fsdp", None),
        P("fsdp"),
        P(None, "fsdp"),
        P("fsdp", "seq", None),
    )
    out_specs = (P("fsdp", "seq", None), P("fsdp", "seq", None), P("fsdp", None), P(None, "fsdp"))
    return jax.shard_map(shards, mesh=mesh, in_specs=in_specs, out_specs=out_specs, check_vma=False)
```

profile of v0, /device:TPU:32, one launch (start us, length us, event | category | flops | bytes accessed | tf_op | source)
XLA Modules:
  0.0 471.1 jit_solution(15271871692152045158)
XLA Ops:
  9.3 0.9 convert_reduce_fusion
  12.2 7.0 %all-to-all-start = ((bf16[16,2,1]{1,2,0:T(2,128)(2,1)}), bf16[16,2,1]{1,2,0:T(2,128)(2,1)S(1)}, u32[]{:S(2)}, u32[]{:S(2)}) async-start(bf16[16,2,1]{1,2,0:T(2,128)(2,1)} %all_to_all.12), calls=%async_computation | async-start | bytes 16384 | tf_op jit(solution)/shard_map/all_to_all | solution.py:113
  19.3 0.7 gather_fusion.5
  20.0 0.7 gather_fusion.6
  20.8 0.7 gather_fusion.8
  21.5 0.7 gather_fusion.7
  23.0 18.3 %all-gather = bf16[16,224,5]{1,2,0:T(8,128)(2,1)S(1)} all-gather(bf16[1,224,5]{1,2,0:T(8,128)(2,1)} %bitcast.126), channel_id=1, replica_groups=mesh['seq'=16,'fsdp'=16] {'fsdp'}, dimensions={0}, use_global_device_ids=true | all-gather | bytes 38080 | tf_op jit(solution)/shard_map/all_gather | solution.py:126
  45.6 0.8 broadcast_multiply_fusion
  46.4 0.9 broadcast_multiply_fusion.1
  47.4 1.8 broadcast_in_dim.19
  49.2 5.8 %scatter_fusion = bf16[32,32,1176]{2,1,0:T(8,128)(2,1)} fusion(bf16[32,32,1176]{2,1,0:T(8,128)(2,1)} %broadcast_in_dim.19, s32[17]{0:T(128)S(1)} %fusion.26, bf16[17,32,1176]{2,1,0:T(8,128)(2,1)S(1)} %bitcast.120), kind=kCustom, calls=%fused_computation.11 | custom fusion | bytes 3838532 | tf_op jit(solution)/shard_map/scatter | solution.py:103
  55.0 7.3 %all-to-all-start.1 = ((bf16[32,32,1176]{2,1,0:T(8,128)(2,1)}), bf16[32,32,1176]{2,1,0:T(8,128)(2,1)}, u32[]{:S(2)}, u32[]{:S(2)}) async-start(bf16[32,32,1176]{2,1,0:T(8,128)(2,1)} %scatter_fusion), calls=%async_computation.1 | async-start | bytes 5242880 | tf_op jit(solution)/shard_map/all_to_all | solution.py:112
  63.9 24.1 %all-reduce = bf16[3584]{0:T(1024)(128)(2,1)S(1)} all-reduce(bf16[3584]{0:T(1024)(128)(2,1)S(1)} %dynamic-update-slice), channel_id=1, replica_groups=mesh['seq'=16,'fsdp'=16] {'fsdp'}, use_global_device_ids=true, to_apply=%add | all-reduce | flops 3584 | bytes 14336
  88.1 1.0 broadcast_multiply_fusion.2
  89.0 1.0 broadcast_multiply_fusion.3
  90.1 8.8 %all-to-all-done.1 = bf16[32,32,1176]{2,1,0:T(8,128)(2,1)} async-done(((bf16[32,32,1176]{2,1,0:T(8,128)(2,1)}), bf16[32,32,1176]{2,1,0:T(8,128)(2,1)}, u32[]{:S(2)}, u32[]{:S(2)}) %all-to-all-start.1) | async-done | bytes 2408480 | tf_op jit(solution)/shard_map/all_to_all | solution.py:112
  99.1 4.2 scatter_fusion.1
  103.4 8.0 %multiply_reduce_fusion.2 = (f32[544]{0:T(1024)S(1)}, f32[544,3584]{1,0:T(8,128)S(1)}) fusion(bf16[544,1176]{1,0:T(8,128)(2,1)S(1)} %bitcast.121, bf16[3584,1176]{1,0:T(8,128)(2,1)} %all-gather.3.cloned.1.call-done), kind=kOutput, calls=%fused_computation.47 | convolution fusion | flops 4589583872 | bytes 17510016 | tf_op jit(solution)/shard_map/dot_general | solution.py:130
  111.5 1.3 multiply_convert_fusion
  112.9 1.6 collective-permute-start.1
  114.5 4.8 %collective-permute-start = (bf16[64,3584]{1,0:T(8,128)(2,1)S(1)}, bf16[64,3584]{1,0:T(8,128)(2,1)S(1)}, u32[]{:S(2)}, u32[]{:S(2)}) collective-permute-start(bf16[64,3584]{1,0:T(8,128)(2,1)S(1)} %get-tuple-element.46), channel_id=1, source_target_pairs={{0,16},{16,32},{32,48},{48,64},{64,80},{80,96},{96,112},{112,128},... | collective-permute-start | bytes 1376264 | tf_op jit(solution)/shard_map/ppermute | solution.py:18
  119.3 0.9 broadcast_multiply_fusion.4
  120.2 5.8 %collective-permute-done.1 = bf16[64,3584]{1,0:T(8,128)(2,1)S(1)} collective-permute-done((bf16[64,3584]{1,0:T(8,128)(2,1)S(1)}, bf16[64,3584]{1,0:T(8,128)(2,1)S(1)}, u32[]{:S(2)}, u32[]{:S(2)}) %collective-permute-start.1) | collective-permute-done | bytes 458784 | tf_op jit(solution)/shard_map/ppermute | solution.py:20
  126.0 1.3 collective-permute-done
  127.4 8.3 %convert_multiply_fusion = (f32[544,3584]{1,0:T(8,128)}, bf16[544,3584]{1,0:T(8,128)(2,1)S(1)}, f32[544,3584]{1,0:T(8,128)}) fusion(bf16[64,3584]{1,0:T(8,128)(2,1)S(1)} %collective-permute-done.1, bf16[544,3584]{1,0:T(8,128)(2,1)S(1)} %multiply_convert_fusion, bf16[1,544,3584]{2,1,0:T(8,128)(2,1)S(1)} %copy-done.5, f32[17,3584]{1,0:T(8,128)S(1)} %copy-done.7, ...), kind=kLoop, calls=%fused_computation.13 | loop fusion | flops 74088448 | bytes 29431808 | tf_op jit(solution)/shard_map/mul | solution.py:72
  135.7 1.9 copy-done.3
  137.6 0.8 fusion.45
  138.4 5.5 %collective-permute-start.3 = (bf16[64,3584]{1,0:T(8,128)(2,1)}, bf16[64,3584]{1,0:T(8,128)(2,1)}, u32[]{:S(2)}, u32[]{:S(2)}) collective-permute-start(bf16[64,3584]{1,0:T(8,128)(2,1)} %get-tuple-element.45), channel_id=1, source_target_pairs={{0,16},{16,32},{32,48},{48,64},{64,80},{80,96},{96,112},{112,128},... | collective-permute-start | bytes 1376264 | tf_op jit(solution)/shard_map/ppermute | solution.py:18
  143.9 1.5 collective-permute-start.2
  145.4 15.1 %convert_multiply_fusion.1 = (f32[544,3584]{1,0:T(8,128)}, f32[544,3584]{1,0:T(8,128)}, f32[544,3584]{1,0:T(8,128)}, f32[544,3584]{1,0:T(8,128)}) fusion(bf16[544,3584]{1,0:T(8,128)(2,1)} %copy-done.3, bf16[64,3584]{1,0:T(8,128)(2,1)S(1)} %collective-permute-done.1, bf16[544,3584]{1,0:T(8,128)(2,1)} %copy-done.4, bf16[64,3584]{1,0:T(8,128)(2,1)S(1)} %collective-permute-done), kind=kLoop, calls=%fused_computation.14 | loop fusion | flops 35094528 | bytes 39911424 | tf_op jit(solution)/shard_map/mul | solution.py:72
  160.5 4.3 reduce_sum.133
  165.0 4.4 reduce_sum.135
  169.5 4.4 reduce_sum.137
  174.0 4.4 reduce_sum.139
  178.5 4.4 reduce_sum.141
  183.0 10.2 %fusion.9 = f32[544,3584]{1,0:T(8,128)S(1)} fusion(bf16[544,3584]{1,0:T(8,128)(2,1)} %copy-done.3, bf16[64,3584]{1,0:T(8,128)(2,1)} %collective-permute-done.3, bf16[64,3584]{1,0:T(8,128)(2,1)} %collective-permute-done.2, f32[17,3584]{1,0:T(8,128)S(1)} %get-tuple-element.56, f32[17,3584]{1,0:T(8,128)} %get-tuple-element.54, ...), kind=kLoop, calls=%fused_computation.36 | loop fusion | flops 50692096 | bytes 13834240 | tf_op jit(solution)/shard_map/add | solution.py:62
  193.3 2.1 multiply_reduce_fusion
  195.4 9.9 %fusion.6 = (bf16[544,3584]{1,0:T(8,128)(2,1)}, bf16[1,544,3584]{2,1,0:T(8,128)(2,1)}) fusion(f32[544,3584]{1,0:T(8,128)S(1)} %fusion.9, f32[544,3584]{1,0:T(8,128)S(1)} %bitcast.114, bf16[1,544,3584]{2,1,0:T(8,128)(2,1)} %param.13, f32[544]{0:T(1024)S(1)} %broadcast_multiply_fusion.10, f32[3584]{0:T(1024)S(1)} %convert_element_type.185, ...), kind=kLoop, calls=%fused_computation.33 | loop fusion | flops 27295744 | bytes 35113216 | tf_op jit(solution)/shard_map/convert_element_type | solution.py:157
  205.3 12.7 %fusion.47 = f32[3584,1176]{0,1:T(8,128)} fusion(bf16[544,3584]{1,0:T(8,128)(2,1)} %get-tuple-element.42, bf16[544,1176]{1,0:T(8,128)(2,1)S(1)} %bitcast.122), kind=kOutput, calls=%fused_computation.172 | convolution fusion | flops 4585684992 | bytes 22038016 | tf_op jit(solution)/shard_map/dot_general | solution.py:165
  218.1 11.5 %pad_maximum_fusion = f32[3584,1182]{0,1:T(8,128)} fusion(f32[3584,6]{0,1:T(8,128)S(1)} %bitcast.123, f32[3584,1176]{0,1:T(8,128)} %fusion.47), kind=kLoop, calls=%fused_computation.19 | loop fusion | flops 4236288 | bytes 33890304 | tf_op jit(solution)/shard_map/concatenate | solution.py:169
  229.6 18.8 %copy.23 = f32[3584,1182]{1,0:T(8,128)} copy(f32[3584,1182]{0,1:T(8,128)} %pad_maximum_fusion) | data formatting | bytes 33890304
  248.5 109.9 %reduce-scatter.4.cloned.1.call-done = f32[224,1182]{1,0:T(8,128)} async-done(((f32[3584,1182]{1,0:T(8,128)}), f32[224,1182]{1,0:T(8,128)}) %reduce-scatter.4.cloned.1.call-update) | async-done | bytes 1059088
  358.4 2.7 copy.24
  361.1 10.4 %fusion.16 = bf16[1,544,1176]{2,1,0:T(8,128)(2,1)} fusion(bf16[544,3584]{1,0:T(8,128)(2,1)} %get-tuple-element.42, bf16[3584,1176]{1,0:T(8,128)(2,1)} %all-gather.3.cloned.1.call-done), kind=kOutput, calls=%fused_computation.66 | convolution fusion | flops 4586324992 | bytes 13608448 | tf_op jit(solution)/shard_map/dot_general | solution.py:158
  371.5 89.3 %all-reduce.3.cloned.1.call-done = f32[224,1182]{0,1:T(8,128)} async-done(((f32[224,1182]{0,1:T(8,128)}), f32[224,1182]{0,1:T(8,128)}) %all-reduce.3.cloned.1.call-update) | async-done | bytes 1059088 | tf_op jit(solution)/shard_map/psum | solution.py:171
  460.8 1.4 fusion.17
  462.2 1.0 copy.22
  463.3 1.3 fusion.18
  (107 shorter events, 11.4 us)
Async XLA Ops:
  7.2 12.1 %copy-start = (s32[1,272]{1,0:T(1,128)S(1)}, s32[1,272]{1,0:T(1,128)}, u32[]{:S(2)}) copy-start(s32[1,272]{1,0:T(1,128)} %param.9) | copy-start | bytes 3268
  7.2 42.0 %copy-start.6 = (bf16[1,544,1176]{2,1,0:T(8,128)(2,1)S(1)}, bf16[1,544,1176]{2,1,0:T(8,128)(2,1)}, u32[]{:S(2)}) copy-start(bf16[1,544,1176]{2,1,0:T(8,128)(2,1)} %param.7) | copy-start | bytes 3838468
  7.2 96.2 %all-gather.3.cloned.1.call-start = ((), (), s32[]{:S(2)}) async-start(), calls=%async_computation.3 | async-start | bytes 9748480 | tf_op jit(solution)/shard_map/all_gather | solution.py:124
  12.2 42.8 %all-to-all-start = ((bf16[16,2,1]{1,2,0:T(2,128)(2,1)}), bf16[16,2,1]{1,2,0:T(2,128)(2,1)S(1)}, u32[]{:S(2)}, u32[]{:S(2)}) async-start(bf16[16,2,1]{1,2,0:T(2,128)(2,1)} %all_to_all.12), calls=%async_computation | async-start | bytes 16384 | tf_op jit(solution)/shard_map/all_to_all | solution.py:113
  42.2 20.2 %copy-start.12 = (u32[256]{0:T(256)S(1)}, u32[256]{0:T(256)}, u32[]{:S(2)}) copy-start(u32[256]{0:T(256)} %constant.79) | copy-start | bytes 3076
  42.2 21.5 %copy-start.11 = (bf16[224]{0:T(256)(128)(2,1)S(1)}, bf16[224]{0:T(256)(128)(2,1)}, u32[]{:S(2)}) copy-start(bf16[224]{0:T(256)(128)(2,1)} %param.11) | copy-start | bytes 1348
  55.0 43.9 %all-to-all-start.1 = ((bf16[32,32,1176]{2,1,0:T(8,128)(2,1)}), bf16[32,32,1176]{2,1,0:T(8,128)(2,1)}, u32[]{:S(2)}, u32[]{:S(2)}) async-start(bf16[32,32,1176]{2,1,0:T(8,128)(2,1)} %scatter_fusion), calls=%async_computation.1 | async-start | bytes 5242880 | tf_op jit(solution)/shard_map/all_to_all | solution.py:112
  62.3 296.1 %reduce-scatter.4.cloned.1.call-start = ((), (), s32[]{:S(2)}) async-start(), calls=%async_computation.5 | async-start | bytes 19496960
  111.4 24.2 %copy-start.2 = (f32[544,3584]{1,0:T(8,128)}, f32[544,3584]{1,0:T(8,128)S(1)}, u32[]{:S(2)}) copy-start(f32[544,3584]{1,0:T(8,128)S(1)} %get-tuple-element.69) | copy-start | bytes 23396356
  111.4 15.9 %copy-start.5 = (bf16[1,544,3584]{2,1,0:T(8,128)(2,1)S(1)}, bf16[1,544,3584]{2,1,0:T(8,128)(2,1)}, u32[]{:S(2)}) copy-start(bf16[1,544,3584]{2,1,0:T(8,128)(2,1)} %param.13) | copy-start | bytes 11698180
  111.5 15.9 %copy-start.7 = (f32[17,3584]{1,0:T(8,128)S(1)}, f32[17,3584]{1,0:T(8,128)}, u32[]{:S(2)}) copy-start(f32[17,3584]{1,0:T(8,128)} %get-tuple-element.57) | copy-start | bytes 731140
  111.5 15.9 %copy-start.8 = (f32[17,3584]{1,0:T(8,128)S(1)}, f32[17,3584]{1,0:T(8,128)}, u32[]{:S(2)}) copy-start(f32[17,3584]{1,0:T(8,128)} %get-tuple-element.55) | copy-start | bytes 731140
  111.5 15.9 %copy-start.9 = (f32[17,3584]{1,0:T(8,128)S(1)}, f32[17,3584]{1,0:T(8,128)}, u32[]{:S(2)}) copy-start(f32[17,3584]{1,0:T(8,128)} %get-tuple-element.53) | copy-start | bytes 731140
  111.5 15.9 %copy-start.10 = (f32[17,3584]{1,0:T(8,128)S(1)}, f32[17,3584]{1,0:T(8,128)}, u32[]{:S(2)}) copy-start(f32[17,3584]{1,0:T(8,128)} %get-tuple-element.51) | copy-start | bytes 731140
  112.8 22.9 %copy-start.4 = (bf16[544,3584]{1,0:T(8,128)(2,1)}, bf16[544,3584]{1,0:T(8,128)(2,1)S(1)}, u32[]{:S(2)}) copy-start(bf16[544,3584]{1,0:T(8,128)(2,1)S(1)} %multiply_convert_fusion) | copy-start | bytes 11698180
  112.9 13.1 %collective-permute-start.1 = (bf16[64,3584]{1,0:T(8,128)(2,1)S(1)}, bf16[64,3584]{1,0:T(8,128)(2,1)S(1)}, u32[]{:S(2)}, u32[]{:S(2)}) collective-permute-start(bf16[64,3584]{1,0:T(8,128)(2,1)S(1)} %get-tuple-element.47), channel_id=1, source_target_pairs={{16,0},{32,16},{48,32},{64,48},{80,64},{96,80},{112,96},{128,112},... | collective-permute-start | bytes 1376264 | tf_op jit(solution)/shard_map/ppermute | solution.py:20
  114.5 12.9 %collective-permute-start = (bf16[64,3584]{1,0:T(8,128)(2,1)S(1)}, bf16[64,3584]{1,0:T(8,128)(2,1)S(1)}, u32[]{:S(2)}, u32[]{:S(2)}) collective-permute-start(bf16[64,3584]{1,0:T(8,128)(2,1)S(1)} %get-tuple-element.46), channel_id=1, source_target_pairs={{0,16},{16,32},{32,48},{48,64},{64,80},{80,96},{96,112},{112,128},... | collective-permute-start | bytes 1376264 | tf_op jit(solution)/shard_map/ppermute | solution.py:18
  135.7 1.9 copy-start.3
  138.4 44.6 %collective-permute-start.3 = (bf16[64,3584]{1,0:T(8,128)(2,1)}, bf16[64,3584]{1,0:T(8,128)(2,1)}, u32[]{:S(2)}, u32[]{:S(2)}) collective-permute-start(bf16[64,3584]{1,0:T(8,128)(2,1)} %get-tuple-element.45), channel_id=1, source_target_pairs={{0,16},{16,32},{32,48},{48,64},{64,80},{80,96},{96,112},{112,128},... | collective-permute-start | bytes 1376264 | tf_op jit(solution)/shard_map/ppermute | solution.py:18
  143.9 39.1 %collective-permute-start.2 = (bf16[64,3584]{1,0:T(8,128)(2,1)S(1)}, bf16[64,3584]{1,0:T(8,128)(2,1)}, u32[]{:S(2)}, u32[]{:S(2)}) collective-permute-start(bf16[64,3584]{1,0:T(8,128)(2,1)S(1)} %get-tuple-element.44), channel_id=1, source_target_pairs={{16,0},{32,16},{48,32},{64,48},{80,64},{96,80},{112,96},{128,112},... | collective-permute-start | bytes 1376264 | tf_op jit(solution)/shard_map/ppermute | solution.py:20
  182.8 10.4 %slice-start = ((s8[7798784]{0:T(1024)(128)(4,1)}), s8[4194304]{0:T(1024)(128)(4,1)S(1)}, s32[]{:S(2)}) async-start(s8[7798784]{0:T(1024)(128)(4,1)} %bitcast.113), calls=%async_computation.6 | async-start | bytes 8388608
  183.0 10.3 %slice-start.1 = ((s8[7798784]{0:T(1024)(128)(4,1)}), s8[3604480]{0:T(1024)(128)(4,1)S(1)}, s32[]{:S(2)}) async-start(s8[7798784]{0:T(1024)(128)(4,1)} %bitcast.113), calls=%async_computation.7 | async-start | bytes 7208960
  248.5 212.3 %all-reduce.3.cloned.1.call-start = ((), (), s32[]{:S(2)}) async-start(), calls=%async_computation.4 | async-start | bytes 2424832 | tf_op jit(solution)/shard_map/psum | solution.py:171
  361.1 103.5 %copy-start.1 = (s32[1,272]{1,0:T(1,128)S(1)}, s32[1,272]{1,0:T(1,128)}, u32[]{:S(2)}) copy-start(s32[1,272]{1,0:T(1,128)} %param.9) | copy-start | bytes 3268
Sparse Core Ops, SparseCore 0:
  9.9 60.7 all-gather.2
  248.6 109.7 reduce-scatter.3
  361.7 99.0 all-reduce.2
where the time goes:
time: 472 us; the launch traced here: 471 us
  waiting for transfers between devices  216 us (46%)
  other arithmetic  91.6 us (19%)
  local copies, waits for them, and re-layouts  47.3 us (10%)
  blocking collectives  42.4 us (9%)
  matrix products  31.1 us (7%)
  starting transfers between devices  27.8 us (6%)
  between operations  15 us (3%)
    unnamed x4, waiting for transfers between devices  111 us
    psum x1, waiting for transfers between devices, shards(): summed = lax.psum(grad_shard, 'seq')  89.3 us
    unnamed x36, local copies, waits for them, and re-layouts  25.4 us
    unnamed x1, blocking collectives  24.1 us
    mul x2, other arithmetic, kernel_sums(): slope_blocks.astype(jnp.float32)  23.4 us
    reduce_sum x5, other arithmetic, kernel_sums(): jnp.sum(slope_blocks.astype(jnp.float32) * padded[offset:offset + slot_to...  21.8 us
    all_gather x1, blocking collectives, shards(): lax.all_gather(conv_kernel, 'fsdp', axis=1, tiled=True)  18.3 us
    dot_general x1, matrix products, shards(): lax.dot_general(d_stem_low, packed, (((0,), (0,)), ((), ())), preferred_e...  12.7 us
  transfers between devices with their start and end apart: 9, of which 5 were waited for; matrix products, arithmetic and copies ran while one was open for 16% of the time, Pallas kernels for 0%

commit v1 on v0

--- a/solution.py
+++ b/solution.py
@@ -168,7 +168,7 @@
     grad_shard = lax.psum_scatter(
         jnp.concatenate([weight_block, chan_terms], axis=1), "fsdp", scatter_dimension=0, tiled=True
     )
-    summed = lax.psum(grad_shard, "seq")
+    summed = lax.all_gather(grad_shard, "seq").sum(axis=0)
     grad_scale = 1.0 / math.sqrt(tokens * seq_size * fsdp_size)
     grad_weight = (summed[:, :pixel_width] * grad_scale).astype(jnp.bfloat16)
     grad_channels = (summed[:, pixel_width:] * grad_scale).T

time: 472 us -> 505 us (1.070)
  waiting for transfers between devices: 216 us -> 245 us
  other arithmetic: 91.6 us -> 97.3 us
    all_gather x0 -> x1, waiting for transfers between devices: none -> 118 us  [shards(): summed = lax.all_gather(grad_shard, 'seq').sum(axis=0)]
    unnamed x4 -> x3, waiting for transfers between devices: 111 us -> 0.71 us
    reduce_scatter x0 -> x1, waiting for transfers between devices: none -> 110 us  [shards(): lax.psum_scatter(jnp.concatenate([weight_block, chan_terms], axis=1), 'fs...]
    psum x1 -> x0, waiting for transfers between devices: 89.3 us -> none  [shards(): summed = lax.psum(grad_shard, 'seq')]
    reduce_sum x0 -> x1, other arithmetic: none -> 7.47 us  [shards(): summed = lax.all_gather(grad_shard, 'seq').sum(axis=0)]
    unnamed x36 -> x35, local copies, waits for them, and re-layouts: 25.4 us -> 22.3 us
  transfers between devices with their start and end apart: 9 -> 9, of which waited for: 5 -> 5; matrix products, arithmetic and copies ran while one was open for 16% -> 15% of each run, Pallas kernels for 0% -> 0%
where the time goes in v1:
time: 505 us; the launch traced here: 502 us
  waiting for transfers between devices  245 us (49%)
  other arithmetic  97.3 us (19%)
  local copies, waits for them, and re-layouts  44.2 us (9%)
  blocking collectives  42.4 us (8%)
  matrix products  31.1 us (6%)
  starting transfers between devices  27.8 us (6%)
  between operations  15 us (3%)
    all_gather x1, waiting for transfers between devices, shards(): summed = lax.all_gather(grad_shard, 'seq').sum(axis=0)  118 us
    reduce_scatter x1, waiting for transfers between devices, shards(): lax.psum_scatter(jnp.concatenate([weight_block, chan_terms], axis=1), 'fs...  110 us
    unnamed x1, blocking collectives  24.1 us
    mul x2, other arithmetic, kernel_sums(): slope_blocks.astype(jnp.float32)  23.4 us
    unnamed x35, local copies, waits for them, and re-layouts  22.3 us
    reduce_sum x5, other arithmetic, kernel_sums(): jnp.sum(slope_blocks.astype(jnp.float32) * padded[offset:offset + slot_to...  21.8 us
    all_gather x1, blocking collectives, shards(): lax.all_gather(conv_kernel, 'fsdp', axis=1, tiled=True)  18.3 us
    dot_general x1, matrix products, shards(): lax.dot_general(d_stem_low, packed, (((0,), (0,)), ((), ())), preferred_e...  12.7 us
  transfers between devices with their start and end apart: 9, of which 5 were waited for; matrix products, arithmetic and copies ran while one was open for 15% of the time, Pallas kernels for 0%

profile of v1, /device:TPU:32, one launch (start us, length us, event | category | flops | bytes accessed | tf_op | source)
XLA Modules:
  0.0 502.5 jit_solution(15845633530079855964)
XLA Ops:
  9.3 0.9 convert_reduce_fusion
  12.2 7.0 %all-to-all-start = ((bf16[16,2,1]{1,2,0:T(2,128)(2,1)}), bf16[16,2,1]{1,2,0:T(2,128)(2,1)S(1)}, u32[]{:S(2)}, u32[]{:S(2)}) async-start(bf16[16,2,1]{1,2,0:T(2,128)(2,1)} %all_to_all.12), calls=%async_computation | async-start | bytes 16384 | tf_op jit(solution)/shard_map/all_to_all | solution.py:113
  19.3 0.7 gather_fusion.5
  20.0 0.7 gather_fusion.6
  20.8 0.7 gather_fusion.8
  21.5 0.7 gather_fusion.7
  23.0 18.3 %all-gather.1 = bf16[16,224,5]{1,2,0:T(8,128)(2,1)S(1)} all-gather(bf16[1,224,5]{1,2,0:T(8,128)(2,1)} %bitcast.128), channel_id=1, replica_groups=mesh['seq'=16,'fsdp'=16] {'fsdp'}, dimensions={0}, use_global_device_ids=true | all-gather | bytes 38080 | tf_op jit(solution)/shard_map/all_gather | solution.py:126
  42.9 0.7 gather_fusion.3
  43.7 0.7 gather_fusion.2
  45.6 0.8 broadcast_multiply_fusion
  46.4 0.9 broadcast_multiply_fusion.1
  47.4 1.8 broadcast_in_dim.19
  49.2 5.8 %scatter_fusion = bf16[32,32,1176]{2,1,0:T(8,128)(2,1)} fusion(bf16[32,32,1176]{2,1,0:T(8,128)(2,1)} %broadcast_in_dim.19, s32[17]{0:T(128)S(1)} %fusion.26, bf16[17,32,1176]{2,1,0:T(8,128)(2,1)S(1)} %bitcast.122), kind=kCustom, calls=%fused_computation.11 | custom fusion | bytes 3838532 | tf_op jit(solution)/shard_map/scatter | solution.py:103
  55.0 7.3 %all-to-all-start.1 = ((bf16[32,32,1176]{2,1,0:T(8,128)(2,1)}), bf16[32,32,1176]{2,1,0:T(8,128)(2,1)}, u32[]{:S(2)}, u32[]{:S(2)}) async-start(bf16[32,32,1176]{2,1,0:T(8,128)(2,1)} %scatter_fusion), calls=%async_computation.1 | async-start | bytes 5242880 | tf_op jit(solution)/shard_map/all_to_all | solution.py:112
  63.9 24.1 %all-reduce = bf16[3584]{0:T(1024)(128)(2,1)S(1)} all-reduce(bf16[3584]{0:T(1024)(128)(2,1)S(1)} %dynamic-update-slice), channel_id=1, replica_groups=mesh['seq'=16,'fsdp'=16] {'fsdp'}, use_global_device_ids=true, to_apply=%add | all-reduce | flops 3584 | bytes 14336
  88.1 1.0 broadcast_multiply_fusion.2
  89.0 1.0 broadcast_multiply_fusion.3
  90.1 8.8 %all-to-all-done.1 = bf16[32,32,1176]{2,1,0:T(8,128)(2,1)} async-done(((bf16[32,32,1176]{2,1,0:T(8,128)(2,1)}), bf16[32,32,1176]{2,1,0:T(8,128)(2,1)}, u32[]{:S(2)}, u32[]{:S(2)}) %all-to-all-start.1) | async-done | bytes 2408480 | tf_op jit(solution)/shard_map/all_to_all | solution.py:112
  99.1 4.2 scatter_fusion.1
  103.4 8.0 %multiply_reduce_fusion.2 = (f32[544]{0:T(1024)S(1)}, f32[544,3584]{1,0:T(8,128)S(1)}) fusion(bf16[544,1176]{1,0:T(8,128)(2,1)S(1)} %bitcast.123, bf16[3584,1176]{1,0:T(8,128)(2,1)} %all-gather.5.cloned.1.call-done), kind=kOutput, calls=%fused_computation.47 | convolution fusion | flops 4589583872 | bytes 17510016 | tf_op jit(solution)/shard_map/dot_general | solution.py:130
  111.5 1.3 multiply_convert_fusion
  112.9 1.6 collective-permute-start.1
  114.5 4.8 collective-permute-start
  119.3 0.9 broadcast_multiply_fusion.4
  120.2 5.8 %collective-permute-done.1 = bf16[64,3584]{1,0:T(8,128)(2,1)S(1)} collective-permute-done((bf16[64,3584]{1,0:T(8,128)(2,1)S(1)}, bf16[64,3584]{1,0:T(8,128)(2,1)S(1)}, u32[]{:S(2)}, u32[]{:S(2)}) %collective-permute-start.1) | collective-permute-done | bytes 458784 | tf_op jit(solution)/shard_map/ppermute | solution.py:20
  126.0 1.3 collective-permute-done
  127.4 8.3 %convert_multiply_fusion = (f32[544,3584]{1,0:T(8,128)}, bf16[544,3584]{1,0:T(8,128)(2,1)S(1)}, f32[544,3584]{1,0:T(8,128)}) fusion(bf16[64,3584]{1,0:T(8,128)(2,1)S(1)} %collective-permute-done.1, bf16[544,3584]{1,0:T(8,128)(2,1)S(1)} %multiply_convert_fusion, bf16[1,544,3584]{2,1,0:T(8,128)(2,1)S(1)} %copy-done.5, f32[17,3584]{1,0:T(8,128)S(1)} %copy-done.7, ...), kind=kLoop, calls=%fused_computation.13 | loop fusion | flops 74088448 | bytes 29431808 | tf_op jit(solution)/shard_map/mul | solution.py:72
  135.7 1.9 copy-done.3
  137.6 0.8 fusion.45
  138.4 5.5 %collective-permute-start.3 = (bf16[64,3584]{1,0:T(8,128)(2,1)}, bf16[64,3584]{1,0:T(8,128)(2,1)}, u32[]{:S(2)}, u32[]{:S(2)}) collective-permute-start(bf16[64,3584]{1,0:T(8,128)(2,1)} %get-tuple-element.45), channel_id=1, source_target_pairs={{0,16},{16,32},{32,48},{48,64},{64,80},{80,96},{96,112},{112,128},... | collective-permute-start | bytes 1376264 | tf_op jit(solution)/shard_map/ppermute | solution.py:18
  143.9 1.5 collective-permute-start.2
  145.4 15.1 %convert_multiply_fusion.1 = (f32[544,3584]{1,0:T(8,128)}, f32[544,3584]{1,0:T(8,128)}, f32[544,3584]{1,0:T(8,128)}, f32[544,3584]{1,0:T(8,128)}) fusion(bf16[544,3584]{1,0:T(8,128)(2,1)} %copy-done.3, bf16[64,3584]{1,0:T(8,128)(2,1)S(1)} %collective-permute-done.1, bf16[544,3584]{1,0:T(8,128)(2,1)} %copy-done.4, bf16[64,3584]{1,0:T(8,128)(2,1)S(1)} %collective-permute-done), kind=kLoop, calls=%fused_computation.14 | loop fusion | flops 35094528 | bytes 39911424 | tf_op jit(solution)/shard_map/mul | solution.py:72
  160.5 4.3 reduce_sum.142
  165.0 4.4 reduce_sum.144
  169.5 4.4 reduce_sum.146
  174.0 4.4 reduce_sum.148
  178.5 4.4 reduce_sum.150
  183.0 10.2 %fusion.9 = f32[544,3584]{1,0:T(8,128)S(1)} fusion(bf16[544,3584]{1,0:T(8,128)(2,1)} %copy-done.3, bf16[64,3584]{1,0:T(8,128)(2,1)} %collective-permute-done.3, bf16[64,3584]{1,0:T(8,128)(2,1)} %collective-permute-done.2, f32[17,3584]{1,0:T(8,128)S(1)} %get-tuple-element.56, f32[17,3584]{1,0:T(8,128)} %get-tuple-element.54, ...), kind=kLoop, calls=%fused_computation.36 | loop fusion | flops 50692096 | bytes 13834240 | tf_op jit(solution)/shard_map/add | solution.py:62
  193.3 2.1 multiply_reduce_fusion
  195.4 9.9 %fusion.6 = (bf16[544,3584]{1,0:T(8,128)(2,1)}, bf16[1,544,3584]{2,1,0:T(8,128)(2,1)}) fusion(f32[544,3584]{1,0:T(8,128)S(1)} %fusion.9, f32[544,3584]{1,0:T(8,128)S(1)} %bitcast.115, bf16[1,544,3584]{2,1,0:T(8,128)(2,1)} %param.13, f32[544]{0:T(1024)S(1)} %broadcast_multiply_fusion.10, f32[3584]{0:T(1024)S(1)} %convert_element_type.185, ...), kind=kLoop, calls=%fused_computation.33 | loop fusion | flops 27295744 | bytes 35113216 | tf_op jit(solution)/shard_map/convert_element_type | solution.py:157
  205.3 12.7 %fusion.47 = f32[3584,1176]{0,1:T(8,128)} fusion(bf16[544,3584]{1,0:T(8,128)(2,1)} %get-tuple-element.42, bf16[544,1176]{1,0:T(8,128)(2,1)S(1)} %bitcast.124), kind=kOutput, calls=%fused_computation.172 | convolution fusion | flops 4585684992 | bytes 22038016 | tf_op jit(solution)/shard_map/dot_general | solution.py:165
  218.1 11.5 %pad_maximum_fusion = f32[3584,1182]{0,1:T(8,128)} fusion(f32[3584,6]{0,1:T(8,128)S(1)} %bitcast.125, f32[3584,1176]{0,1:T(8,128)} %fusion.47), kind=kLoop, calls=%fused_computation.19 | loop fusion | flops 4236288 | bytes 33890304 | tf_op jit(solution)/shard_map/concatenate | solution.py:169
  229.6 18.8 %copy.27 = f32[3584,1182]{1,0:T(8,128)} copy(f32[3584,1182]{0,1:T(8,128)} %pad_maximum_fusion) | data formatting | bytes 33890304
  248.4 109.8 %reduce-scatter.4.cloned.1.call-done = f32[224,1182]{1,0:T(8,128)} async-done(((f32[3584,1182]{1,0:T(8,128)}), f32[224,1182]{1,0:T(8,128)}) %reduce-scatter.4.cloned.1.call-update) | async-done | bytes 1059088 | tf_op jit(solution)/shard_map/reduce_scatter | solution.py:168
  358.3 10.4 %fusion.16 = bf16[1,544,1176]{2,1,0:T(8,128)(2,1)} fusion(bf16[544,3584]{1,0:T(8,128)(2,1)} %get-tuple-element.42, bf16[3584,1176]{1,0:T(8,128)(2,1)} %all-gather.5.cloned.1.call-done), kind=kOutput, calls=%fused_computation.66 | convolution fusion | flops 4586324992 | bytes 13608448 | tf_op jit(solution)/shard_map/dot_general | solution.py:158
  368.7 118.0 %all-gather.7.cloned.1.call-done = f32[3584,1182]{1,0:T(8,128)} async-done(((f32[224,1182]{1,0:T(8,128)}), f32[3584,1182]{1,0:T(8,128)}) %all-gather.7.cloned.1.call-update) | async-done | bytes 16945168 | tf_op jit(solution)/shard_map/all_gather | solution.py:171
  486.8 7.5 %reduce_sum.152 = f32[224,1182]{1,0:T(8,128)S(1)} reduce(f32[16,224,1182]{2,1,0:T(8,128)} %bitcast.121, f32[]{:T(128)} %constant.28.clone.1), dimensions={0}, to_apply=%region_18.19 | reduce | flops 3971520 | bytes 18004228 | tf_op jit(solution)/shard_map/reduce_sum | solution.py:171
  494.2 0.9 fusion.17
  (107 shorter events, 10.8 us)
Async XLA Ops:
  7.2 12.1 %copy-start = (s32[1,272]{1,0:T(1,128)S(1)}, s32[1,272]{1,0:T(1,128)}, u32[]{:S(2)}) copy-start(s32[1,272]{1,0:T(1,128)} %param.9) | copy-start | bytes 3268
  7.2 42.0 %copy-start.6 = (bf16[1,544,1176]{2,1,0:T(8,128)(2,1)S(1)}, bf16[1,544,1176]{2,1,0:T(8,128)(2,1)}, u32[]{:S(2)}) copy-start(bf16[1,544,1176]{2,1,0:T(8,128)(2,1)} %param.7) | copy-start | bytes 3838468
  7.2 96.2 %all-gather.5.cloned.1.call-start = ((), (), s32[]{:S(2)}) async-start(), calls=%async_computation.3 | async-start | bytes 9748480 | tf_op jit(solution)/shard_map/all_gather | solution.py:124
  12.2 42.8 %all-to-all-start = ((bf16[16,2,1]{1,2,0:T(2,128)(2,1)}), bf16[16,2,1]{1,2,0:T(2,128)(2,1)S(1)}, u32[]{:S(2)}, u32[]{:S(2)}) async-start(bf16[16,2,1]{1,2,0:T(2,128)(2,1)} %all_to_all.12), calls=%async_computation | async-start | bytes 16384 | tf_op jit(solution)/shard_map/all_to_all | solution.py:113
  42.2 20.2 %copy-start.12 = (u32[256]{0:T(256)S(1)}, u32[256]{0:T(256)}, u32[]{:S(2)}) copy-start(u32[256]{0:T(256)} %constant.79) | copy-start | bytes 3076
  42.2 21.5 %copy-start.11 = (bf16[224]{0:T(256)(128)(2,1)S(1)}, bf16[224]{0:T(256)(128)(2,1)}, u32[]{:S(2)}) copy-start(bf16[224]{0:T(256)(128)(2,1)} %param.11) | copy-start | bytes 1348
  55.0 43.9 %all-to-all-start.1 = ((bf16[32,32,1176]{2,1,0:T(8,128)(2,1)}), bf16[32,32,1176]{2,1,0:T(8,128)(2,1)}, u32[]{:S(2)}, u32[]{:S(2)}) async-start(bf16[32,32,1176]{2,1,0:T(8,128)(2,1)} %scatter_fusion), calls=%async_computation.1 | async-start | bytes 5242880 | tf_op jit(solution)/shard_map/all_to_all | solution.py:112
  62.3 296.0 %reduce-scatter.4.cloned.1.call-start = ((), (), s32[]{:S(2)}) async-start(), calls=%async_computation.5 | async-start | bytes 19496960 | tf_op jit(solution)/shard_map/reduce_scatter | solution.py:168
  111.4 24.2 %copy-start.2 = (f32[544,3584]{1,0:T(8,128)}, f32[544,3584]{1,0:T(8,128)S(1)}, u32[]{:S(2)}) copy-start(f32[544,3584]{1,0:T(8,128)S(1)} %get-tuple-element.69) | copy-start | bytes 23396356
  111.4 15.9 %copy-start.5 = (bf16[1,544,3584]{2,1,0:T(8,128)(2,1)S(1)}, bf16[1,544,3584]{2,1,0:T(8,128)(2,1)}, u32[]{:S(2)}) copy-start(bf16[1,544,3584]{2,1,0:T(8,128)(2,1)} %param.13) | copy-start | bytes 11698180
  111.5 15.9 %copy-start.7 = (f32[17,3584]{1,0:T(8,128)S(1)}, f32[17,3584]{1,0:T(8,128)}, u32[]{:S(2)}) copy-start(f32[17,3584]{1,0:T(8,128)} %get-tuple-element.57) | copy-start | bytes 731140
  111.5 15.9 %copy-start.8 = (f32[17,3584]{1,0:T(8,128)S(1)}, f32[17,3584]{1,0:T(8,128)}, u32[]{:S(2)}) copy-start(f32[17,3584]{1,0:T(8,128)} %get-tuple-element.55) | copy-start | bytes 731140
  111.5 15.9 %copy-start.9 = (f32[17,3584]{1,0:T(8,128)S(1)}, f32[17,3584]{1,0:T(8,128)}, u32[]{:S(2)}) copy-start(f32[17,3584]{1,0:T(8,128)} %get-tuple-element.53) | copy-start | bytes 731140
  111.5 15.9 %copy-start.10 = (f32[17,3584]{1,0:T(8,128)S(1)}, f32[17,3584]{1,0:T(8,128)}, u32[]{:S(2)}) copy-start(f32[17,3584]{1,0:T(8,128)} %get-tuple-element.51) | copy-start | bytes 731140
  112.8 22.9 %copy-start.4 = (bf16[544,3584]{1,0:T(8,128)(2,1)}, bf16[544,3584]{1,0:T(8,128)(2,1)S(1)}, u32[]{:S(2)}) copy-start(bf16[544,3584]{1,0:T(8,128)(2,1)S(1)} %multiply_convert_fusion) | copy-start | bytes 11698180
  112.9 13.1 %collective-permute-start.1 = (bf16[64,3584]{1,0:T(8,128)(2,1)S(1)}, bf16[64,3584]{1,0:T(8,128)(2,1)S(1)}, u32[]{:S(2)}, u32[]{:S(2)}) collective-permute-start(bf16[64,3584]{1,0:T(8,128)(2,1)S(1)} %get-tuple-element.47), channel_id=1, source_target_pairs={{16,0},{32,16},{48,32},{64,48},{80,64},{96,80},{112,96},{128,112},... | collective-permute-start | bytes 1376264 | tf_op jit(solution)/shard_map/ppermute | solution.py:20
  114.5 12.9 %collective-permute-start = (bf16[64,3584]{1,0:T(8,128)(2,1)S(1)}, bf16[64,3584]{1,0:T(8,128)(2,1)S(1)}, u32[]{:S(2)}, u32[]{:S(2)}) collective-permute-start(bf16[64,3584]{1,0:T(8,128)(2,1)S(1)} %get-tuple-element.46), channel_id=1, source_target_pairs={{0,16},{16,32},{32,48},{48,64},{64,80},{80,96},{96,112},{112,128},... | collective-permute-start | bytes 1376264 | tf_op jit(solution)/shard_map/ppermute | solution.py:18
  135.7 1.9 copy-start.3
  138.4 44.6 %collective-permute-start.3 = (bf16[64,3584]{1,0:T(8,128)(2,1)}, bf16[64,3584]{1,0:T(8,128)(2,1)}, u32[]{:S(2)}, u32[]{:S(2)}) collective-permute-start(bf16[64,3584]{1,0:T(8,128)(2,1)} %get-tuple-element.45), channel_id=1, source_target_pairs={{0,16},{16,32},{32,48},{48,64},{64,80},{80,96},{96,112},{112,128},... | collective-permute-start | bytes 1376264 | tf_op jit(solution)/shard_map/ppermute | solution.py:18
  143.9 39.1 %collective-permute-start.2 = (bf16[64,3584]{1,0:T(8,128)(2,1)S(1)}, bf16[64,3584]{1,0:T(8,128)(2,1)}, u32[]{:S(2)}, u32[]{:S(2)}) collective-permute-start(bf16[64,3584]{1,0:T(8,128)(2,1)S(1)} %get-tuple-element.44), channel_id=1, source_target_pairs={{16,0},{32,16},{48,32},{64,48},{80,64},{96,80},{112,96},{128,112},... | collective-permute-start | bytes 1376264 | tf_op jit(solution)/shard_map/ppermute | solution.py:20
  182.8 10.4 %slice-start = ((s8[7798784]{0:T(1024)(128)(4,1)}), s8[4194304]{0:T(1024)(128)(4,1)S(1)}, s32[]{:S(2)}) async-start(s8[7798784]{0:T(1024)(128)(4,1)} %bitcast.114), calls=%async_computation.6 | async-start | bytes 8388608
  183.0 10.3 %slice-start.1 = ((s8[7798784]{0:T(1024)(128)(4,1)}), s8[3604480]{0:T(1024)(128)(4,1)S(1)}, s32[]{:S(2)}) async-start(s8[7798784]{0:T(1024)(128)(4,1)} %bitcast.114), calls=%async_computation.7 | async-start | bytes 7208960
  248.4 238.4 %all-gather.7.cloned.1.call-start = ((), (), s32[]{:S(2)}) async-start(), calls=%async_computation.4 | async-start | bytes 19496960 | tf_op jit(solution)/shard_map/all_gather | solution.py:171
  486.8 9.2 %copy-start.1 = (s32[1,272]{1,0:T(1,128)S(1)}, s32[1,272]{1,0:T(1,128)}, u32[]{:S(2)}) copy-start(s32[1,272]{1,0:T(1,128)} %param.9) | copy-start | bytes 3268
Sparse Core Ops, SparseCore 0:
  9.9 60.7 all-gather.4
  248.5 109.7 reduce-scatter.3
  360.8 125.9 all-gather.6
